TPU v7x, 128 devices: a whole 4x4x4 slice. The times are simulated.
128 devices in a mesh: dp: 16 (over z, x_lo, core), ctx: 8 (over x_hi, y).
Axes of the slice: x: 4 (x_hi: 2, x_lo: 2; x = x_hi * 2 + x_lo), y: 4, z: 4, core: 2. Of those that a mesh axis runs over, the one named last changes fastest.
Arguments:
- hidden: bfloat16 [16, 1024, 4096], P('dp', 'ctx'), may hold values from -6 to 6
- queries: bfloat16 [16, 1024, 4096], P('dp', 'ctx'), may hold values from -6 to 6
- keys: bfloat16 [16, 1024, 256], P('dp', 'ctx'), may hold values from -6 to 6
- values: bfloat16 [16, 1024, 256], P('dp', 'ctx'), may hold values from -24 to 24
- out_weight: bfloat16 [4096, 4096], P(None, 'ctx'), may hold values from -0.09375 to 0.09375
- norm_gain: float32 [4096], replicated, may hold values from 0.1 to 1.9
- routes: int32 [16, 1024, 8], P('dp', 'ctx'), may hold values from 0 to 127, all different within a row; in each aligned block of 128 rows (0 to 127, 128 to 255, ..., all dimensions but the last counted through in order) at most 9 rows name the same one
- slot_scores: float32 [16, 1024, 8], P('dp', 'ctx'), may hold values from 0.1 to 1
- gate_weight: bfloat16 [128, 4096, 768], P(('dp', 'ctx')), may hold values from -0.09375 to 0.09375
- up_weight: bfloat16 [128, 4096, 768], P(('dp', 'ctx')), may hold values from -0.09375 to 0.09375
- down_weight: bfloat16 [128, 768, 4096], P(('dp', 'ctx')), may hold values from -0.21875 to 0.21875
Outputs:
- output: bfloat16 [16, 1024, 4096], P('dp', 'ctx')
Inputs may be any that keep to these rules, and one draw needn't show every extreme that they name: In each aligned block of 128 tokens (the tokens of one device, sequences in order) no expert is named by more than 9 of the block's routes, a bound that some block reaches.
All inputs are finite; a program needn't handle non-finite values.
Results may differ from a plain program's by a relative error of at most 0.0065.
Values may be sent and summed in bfloat16 or wider, within the bound.
No kernel may reach another device: no remote copies, remote signals or barrier semaphores. Data moves between devices by JAX's collectives and lax.ppermute only.
A program may use at most 192 MiB of HBM per device.

v0:
```python
import jax
import jax.numpy as jnp
from jax import lax
from jax.sharding import PartitionSpec as P

HQ = 32
KVH = 2
DH = 128
TOP = 8


def expert_ffn(slots_in, w_gate, w_up, w_down):
    flat_rows = slots_in.reshape(-1, slots_in.shape[-1])
    gated = jnp.dot(flat_rows, w_gate, preferred_element_type=jnp.float32)
    lifted = jnp.dot(flat_rows, w_up, preferred_element_type=jnp.float32)
    activated = (jax.nn.silu(gated) * lifted).astype(jnp.bfloat16)
    result = jnp.dot(activated, w_down, preferred_element_type=jnp.float32).astype(jnp.bfloat16)
    return result.reshape(slots_in.shape)


def local(
    hidden,
    queries,
    keys,
    values,
    out_weight,
    norm_gain,
    routes,
    slot_scores,
    gate_weight,
    up_weight,
    down_weight,
):
    tok_count = hidden.shape[1]
    model_width = hidden.shape[2]
    group_size = HQ // KVH
    score_scale = DH ** (-0.5)
    ctx_index = lax.axis_index("ctx")
    query_rows = queries[0].reshape(tok_count, KVH, group_size, DH)
    query_pos = ctx_index * tok_count + jnp.arange(tok_count, dtype=jnp.int32)
    key_piece = lax.all_gather(keys, "ctx", axis=1, tiled=True)
    value_piece = lax.all_gather(values, "ctx", axis=1, tiled=True)
    key_count = key_piece.shape[1]
    key_rows = key_piece[0].reshape(key_count, KVH, DH)
    value_rows = value_piece[0].reshape(key_count, KVH, DH)
    key_pos = jnp.arange(key_count, dtype=jnp.int32)
    running_max = jnp.full((KVH, group_size, tok_count), -1e30, jnp.float32)
    scores = (
        jnp.einsum("qkgd,jkd->kgqj", query_rows, key_rows, preferred_element_type=jnp.float32)
        * score_scale
    )
    causal = key_pos[None, :] <= query_pos[:, None]
    scores = jnp.where(causal, scores, -1e30)
    new_max = jnp.maximum(running_max, jnp.max(scores, axis=-1))
    weights = jnp.where(causal, jnp.exp(scores - new_max[..., None]), 0.0)
    running_sum = jnp.sum(weights, axis=-1)
    numerator = jnp.einsum(
        "kgqj,jkd->kgqd",
        weights.astype(jnp.bfloat16),
        value_rows,
        preferred_element_type=jnp.float32,
    )
    running_max, running_sum, numerator = (new_max, running_sum, numerator)
    attended = numerator / running_sum[..., None]
    attended = (
        jnp.transpose(attended, (2, 0, 1, 3)).reshape(tok_count, HQ * DH).astype(jnp.bfloat16)
    )
    columns = jnp.dot(
        lax.all_gather(attended, "ctx", axis=0, tiled=True),
        out_weight,
        preferred_element_type=jnp.float32,
    ).astype(jnp.bfloat16)
    projected = lax.all_to_all(columns, "ctx", split_axis=0, concat_axis=1, tiled=True)
    residual = hidden[0].astype(jnp.float32) + projected.astype(jnp.float32)
    normed = (
        residual
        * lax.rsqrt(jnp.mean(residual * residual, axis=1, keepdims=True) + 1e-06)
        * norm_gain
    ).astype(jnp.bfloat16)
    score_rows = slot_scores[0]
    slot_gates = score_rows / jnp.sum(score_rows, axis=1, keepdims=True)
    expert_total = lax.axis_size(("dp", "ctx"))
    capacity = max(2, tok_count * TOP * 9 // (8 * expert_total))
    expert_ids = routes[0].reshape(tok_count * TOP)
    one_hot = (expert_ids[:, None] == jnp.arange(expert_total, dtype=jnp.int32)[None, :]).astype(
        jnp.int32
    )
    earlier = jnp.sum((jnp.cumsum(one_hot, axis=0) - one_hot) * one_hot, axis=1)
    slot_index = expert_ids * capacity + earlier
    token_of = jnp.arange(tok_count * TOP, dtype=jnp.int32) // TOP
    outgoing = (
        jnp.zeros((expert_total * capacity, model_width), jnp.bfloat16)
        .at[slot_index]
        .set(normed[token_of])
    )
    outgoing = outgoing.reshape(expert_total, capacity, model_width)
    served = expert_ffn(
        lax.all_to_all(outgoing, ("dp", "ctx"), split_axis=0, concat_axis=0, tiled=True),
        gate_weight[0],
        up_weight[0],
        down_weight[0],
    )
    returned = lax.all_to_all(served, ("dp", "ctx"), split_axis=0, concat_axis=0, tiled=True)
    returned = returned.reshape(expert_total * capacity, model_width)
    picked = returned[slot_index].reshape(tok_count, TOP, model_width)
    mixture = jnp.sum(slot_gates[:, :, None] * picked.astype(jnp.float32), axis=1)
    return (residual + mixture).astype(jnp.bfloat16)[None]


def solution(mesh):
    return jax.shard_map(
        local,
        mesh=mesh,
        in_specs=(
            P("dp", "ctx", None),
            P("dp", "ctx", None),
            P("dp", "ctx", None),
            P("dp", "ctx", None),
            P(None, "ctx"),
            P(),
            P("dp", "ctx", None),
            P("dp", "ctx", None),
            P(("dp", "ctx"), None, None),
            P(("dp", "ctx"), None, None),
            P(("dp", "ctx"), None, None),
        ),
        out_specs=P("dp", "ctx", None),
        check_vma=False,
    )
```

profile of v0, /device:TPU:91, one launch (start us, length us, event | category | flops | bytes accessed | tf_op | source)
XLA Modules:
  0.0 829.0 jit_solution(7543872358024971029)
XLA Ops:
  6.5 0.0 all-gather.2.cloned.1.call-start
  6.5 29.6 %all_gather.10 = bf16[1,1024,256]{2,1,0:T(8,128)(2,1)S(1)} all-gather(bf16[1,128,256]{2,1,0:T(8,128)(2,1)} %param.14), channel_id=1, replica_groups=mesh['dp'=16,'ctx'=8] {'ctx'}, dimensions={1}, use_global_device_ids=true | all-gather | bytes 589824 | tf_op jit(solution)/shard_map/all_gather | solution.py:42
  36.2 0.2 copy.21
  36.4 0.1 iota_compare_fusion.2
  36.5 1.0 copy.18
  37.5 25.4 %all_gather.9 = bf16[1,1024,256]{1,2,0:T(8,128)(2,1)S(1)} all-gather(bf16[1,128,256]{1,2,0:T(8,128)(2,1)S(1)} %copy.18), channel_id=1, replica_groups=mesh['dp'=16,'ctx'=8] {'ctx'}, dimensions={1}, use_global_device_ids=true | all-gather | bytes 589824 | tf_op jit(solution)/shard_map/all_gather | solution.py:41
  62.9 1.5 copy.37
  64.3 2.9 fusion.1
  67.3 4.1 fusion.2
  71.4 0.0 copy-start.3
  71.4 5.1 fusion.23
  76.6 0.0 all-gather.2.cloned.1.call-update
  76.6 0.0 copy-done.3
  76.6 0.1 copy.26
  76.7 0.1 eq.29
  76.8 0.1 eq.25
  76.9 0.1 copy.25
  77.0 0.1 mul.72
  77.1 0.1 copy.28
  77.2 0.2 fusion.30
  77.4 118.9 %all-gather.2.cloned.1.call-done = bf16[1024,4096]{0,1:T(8,128)(2,1)} async-done(((bf16[128,4096]{0,1:T(8,128)(2,1)}), bf16[1024,4096]{0,1:T(8,128)(2,1)}) %all-gather.2.cloned.1.call-update) | async-done | bytes 8388624 | tf_op jit(solution)/shard_map/all_gather | solution.py:69
  196.4 10.1 %convolution_convert_fusion.1 = bf16[1024,512]{1,0:T(8,128)(2,1)} fusion(bf16[1024,4096]{0,1:T(8,128)(2,1)} %all-gather.2.cloned.1.call-done, bf16[4096,512]{1,0:T(8,128)(2,1)} %param.15), kind=kOutput, calls=%fused_computation.33 | convolution fusion | flops 4295491584 | bytes 13631488 | tf_op jit(solution)/shard_map/dot_general | solution.py:68
  206.4 0.0 copy-start.1
  206.4 0.0 copy-start.2
  206.4 6.2 all-to-all-start
  212.7 0.1 copy.29
  212.8 0.4 fusion.29
  213.2 12.8 %all-to-all-done = bf16[8,128,512]{2,1,0:T(8,128)(2,1)S(1)} async-done(((bf16[8,128,512]{2,1,0:T(8,128)(2,1)}), bf16[8,128,512]{2,1,0:T(8,128)(2,1)S(1)}, u32[]{:S(2)}, u32[]{:S(2)}) %all-to-all-start) | async-done | bytes 1048608 | tf_op jit(solution)/shard_map/all_to_all | solution.py:73
  226.0 1.6 convert_bitcast_fusion
  227.6 0.2 copy.36
  227.9 0.0 copy-done.1
  227.9 0.4 multiply_reduce_fusion
  228.3 0.0 copy-done.2
  228.3 0.4 multiply_convert_fusion
  228.7 7.7 gather_fusion
  236.5 18.4 %scatter_custom_fusion = bf16[1152,4096]{1,0:T(8,128)(2,1)} fusion(s32[1024]{0:T(1024)S(1)} %bitcast.96, bf16[1024,4096]{1,0:T(8,128)(2,1)} %gather_fusion, bf16[]{:T(256)} %constant.43.clone.1), kind=kCustom, calls=%fused_computation.18 | custom fusion | bytes 9437696 | tf_op jit(solution)/shard_map/scatter | solution.py:94
  254.9 15.1 %reshape.163 = bf16[128,9,4096]{2,1,0:T(8,128)(2,1)} reshape(bf16[1152,4096]{1,0:T(8,128)(2,1)} %scatter_custom_fusion) | data formatting | bytes 18874368 | tf_op jit(solution)/shard_map/reshape | solution.py:96
  270.0 197.8 %all_to_all.23 = bf16[128,9,4096]{2,1,0:T(8,128)(2,1)} all-to-all(bf16[128,9,4096]{2,1,0:T(8,128)(2,1)} %reshape.163), channel_id=1, replica_groups=mesh['dp'=16,'ctx'=8] {'dp','ctx'}, dimensions={0} | all-to-all | bytes 18874368 | tf_op jit(solution)/shard_map/all_to_all | solution.py:98
  467.7 15.8 %reshape.164 = bf16[1152,4096]{1,0:T(8,128)(2,1)} reshape(bf16[128,9,4096]{2,1,0:T(8,128)(2,1)} %all_to_all.23) | data formatting | bytes 18874368 | tf_op jit(solution)/shard_map/reshape | solution.py:13
  483.6 0.0 copy-start
  483.6 0.0 slice-start
  483.6 12.0 %fusion.10 = f32[1152,768]{1,0:T(8,128)S(1)} fusion(bf16[1152,4096]{1,0:T(8,128)(2,1)} %reshape.164, bf16[1,4096,768]{2,1,0:T(8,128)(2,1)} %param.19), kind=kOutput, calls=%fused_computation.16 | convolution fusion | flops 7247757312 | bytes 19267584 | tf_op jit(solution)/shard_map/dot_general | solution.py:14
  495.6 0.0 copy-done
  495.6 0.0 slice-start.1
  495.6 10.3 %fusion.17 = bf16[1152,768]{1,0:T(8,128)(2,1)S(1)} fusion(bf16[1152,4096]{1,0:T(8,128)(2,1)S(1)} %copy-done, bf16[1,4096,768]{2,1,0:T(8,128)(2,1)} %param.20, f32[1152,768]{1,0:T(8,128)S(1)} %fusion.10), kind=kOutput, calls=%fused_computation.21 | convolution fusion | flops 7253065728 | bytes 21037056 | tf_op jit(solution)/shard_map/dot_general | solution.py:15
  505.9 0.0 slice-done
  505.9 0.0 slice-done.1
  505.9 9.6 %convolution_convert_fusion = bf16[1152,4096]{1,0:T(8,128)(2,1)} fusion(bf16[1152,768]{1,0:T(8,128)(2,1)S(1)} %fusion.17, bf16[1,768,4096]{2,1,0:T(8,128)(2,1)S(1)} %bitcast.101), kind=kOutput, calls=%fused_computation.7 | convolution fusion | flops 7252475904 | bytes 17498112 | tf_op jit(solution)/shard_map/dot_general | solution.py:17
  515.5 15.1 %reshape.165 = bf16[128,9,4096]{2,1,0:T(8,128)(2,1)} reshape(bf16[1152,4096]{1,0:T(8,128)(2,1)} %convolution_convert_fusion) | data formatting | bytes 18874368 | tf_op jit(solution)/shard_map/reshape | solution.py:18
  530.6 0.0 copy-start.4
  530.6 9.5 %all-to-all-start.2 = ((bf16[128,9,4096]{2,1,0:T(8,128)(2,1)}), bf16[128,9,4096]{2,1,0:T(8,128)(2,1)}, u32[]{:S(2)}, u32[]{:S(2)}) async-start(bf16[128,9,4096]{2,1,0:T(8,128)(2,1)} %reshape.165), calls=%async_computation.2 | async-start | bytes 33554432 | tf_op jit(solution)/shard_map/all_to_all | solution.py:103
  540.1 0.0 copy-done.4
  540.2 0.1 copy.24
  540.3 4.2 copy.23
  544.5 2.7 reshape.167
  547.2 222.0 %all-to-all-done.2 = bf16[128,9,4096]{2,1,0:T(8,128)(2,1)} async-done(((bf16[128,9,4096]{2,1,0:T(8,128)(2,1)}), bf16[128,9,4096]{2,1,0:T(8,128)(2,1)}, u32[]{:S(2)}, u32[]{:S(2)}) %all-to-all-start.2) | async-done | bytes 9437216 | tf_op jit(solution)/shard_map/all_to_all | solution.py:103
  769.3 15.8 %reshape.166 = bf16[1152,4096]{1,0:T(8,128)(2,1)} reshape(bf16[128,9,4096]{2,1,0:T(8,128)(2,1)} %all-to-all-done.2) | data formatting | bytes 18874368 | tf_op jit(solution)/shard_map/reshape | solution.py:104
  785.1 20.0 %gather_fusion.1 = bf16[1024,4096]{1,0:T(8,128)(2,1)} fusion(bf16[1152,4096]{1,0:T(8,128)(2,1)} %reshape.166, s32[1024]{0:T(1024)S(1)} %broadcast_clamp_fusion), kind=kCustom, calls=%fused_computation.1 | custom fusion | bytes 16781312 | tf_op jit(solution)/shard_map/gather | solution.py:105
  805.0 13.2 %fusion = f32[128,4096]{1,0:T(8,128)} fusion(bf16[1024,4096]{1,0:T(8,128)(2,1)} %gather_fusion.1, f32[128,8]{1,0:T(8,128)S(1)} %copy.24), kind=kLoop, calls=%fused_computation.4 | loop fusion | flops 12058624 | bytes 10489856 | tf_op jit(solution)/shard_map/reduce_sum | solution.py:106
  818.2 3.5 fusion.21
  (15 shorter events, 0.1 us)
Async XLA Ops:
  6.5 189.8 %all-gather.2.cloned.1.call-start = ((), (), s32[]{:S(2)}) async-start(), calls=%async_computation.3 | async-start | bytes 9437184 | tf_op jit(solution)/shard_map/all_gather | solution.py:69
  71.4 5.2 copy-start.3
  206.4 21.5 %copy-start.1 = (bf16[1,128,4096]{2,1,0:T(8,128)(2,1)S(1)}, bf16[1,128,4096]{2,1,0:T(8,128)(2,1)}, u32[]{:S(2)}) copy-start(bf16[1,128,4096]{2,1,0:T(8,128)(2,1)} %param.11) | copy-start | bytes 3145732
  206.4 21.9 %copy-start.2 = (f32[4096]{0:T(1024)S(1)}, f32[4096]{0:T(1024)}, u32[]{:S(2)}) copy-start(f32[4096]{0:T(1024)} %param.16) | copy-start | bytes 49156
  206.4 19.6 %all-to-all-start = ((bf16[8,128,512]{2,1,0:T(8,128)(2,1)}), bf16[8,128,512]{2,1,0:T(8,128)(2,1)S(1)}, u32[]{:S(2)}, u32[]{:S(2)}) async-start(bf16[8,128,512]{2,1,0:T(8,128)(2,1)} %bitcast.93), calls=%async_computation | async-start | bytes 2097152 | tf_op jit(solution)/shard_map/all_to_all | solution.py:73
  483.6 12.0 %copy-start = (bf16[1152,4096]{1,0:T(8,128)(2,1)S(1)}, bf16[1152,4096]{1,0:T(8,128)(2,1)}, u32[]{:S(2)}) copy-start(bf16[1152,4096]{1,0:T(8,128)(2,1)} %reshape.164) | copy-start | bytes 28311556
  483.6 22.3 %slice-start = ((s8[6291456]{0:T(1024)(128)(4,1)}), s8[4194304]{0:T(1024)(128)(4,1)S(1)}, s32[]{:S(2)}) async-start(s8[6291456]{0:T(1024)(128)(4,1)} %bitcast.100), calls=%async_computation.4 | async-start | bytes 8388608
  495.6 10.3 %slice-start.1 = ((s8[6291456]{0:T(1024)(128)(4,1)}), s8[2097152]{0:T(1024)(128)(4,1)S(1)}, s32[]{:S(2)}) async-start(s8[6291456]{0:T(1024)(128)(4,1)} %bitcast.100), calls=%async_computation.5 | async-start | bytes 4194304
  530.6 9.6 %copy-start.4 = (f32[1,128,8]{1,2,0:T(8,128)S(1)}, f32[1,128,8]{1,2,0:T(8,128)}, u32[]{:S(2)}) copy-start(f32[1,128,8]{1,2,0:T(8,128)} %param.18) | copy-start | bytes 12292
  530.6 238.7 %all-to-all-start.2 = ((bf16[128,9,4096]{2,1,0:T(8,128)(2,1)}), bf16[128,9,4096]{2,1,0:T(8,128)(2,1)}, u32[]{:S(2)}, u32[]{:S(2)}) async-start(bf16[128,9,4096]{2,1,0:T(8,128)(2,1)} %reshape.165), calls=%async_computation.2 | async-start | bytes 33554432 | tf_op jit(solution)/shard_map/all_to_all | solution.py:103
Sparse Core Ops, SparseCore 0:
  76.7 119.6 all-gather.1
where the time goes:
time: 839 us; the launch traced here: 829 us
  waiting for transfers between devices  354 us (42%)
  blocking collectives  253 us (30%)
  local copies, waits for them, and re-layouts  119 us (14%)
  matrix products  49.9 us (6%)
  other arithmetic  24.1 us (3%)
  starting transfers between devices  15.8 us (2%)
  between operations  14.1 us (2%)
    all_to_all x1, waiting for transfers between devices, local(): lax.all_to_all(served, ('dp', 'ctx'), split_axis=0, concat_axis=0, tiled=...  222 us
    all_to_all x1, blocking collectives, local(): lax.all_to_all(outgoing, ('dp', 'ctx'), split_axis=0, concat_axis=0, tile...  198 us
    all_gather x1, waiting for transfers between devices, local(): lax.all_gather(attended, 'ctx', axis=0, tiled=True)  119 us
    all_gather x1, blocking collectives, local(): value_piece = lax.all_gather(values, 'ctx', axis=1, tiled=True)  29.6 us
    all_gather x1, blocking collectives, local(): key_piece = lax.all_gather(keys, 'ctx', axis=1, tiled=True)  25.4 us
    gather x1, local copies, waits for them, and re-layouts, local(): picked = returned[slot_index].reshape(tok_count, TOP, model_width)  20 us
    scatter x1, local copies, waits for them, and re-layouts, local(): outgoing = jnp.zeros((expert_total * capacity, model_width), jnp.bfloat16...  18.4 us
  transfers between devices with their start and end apart: 3, of which 3 were waited for; matrix products, arithmetic and copies ran while one was open for 1% of the time, Pallas kernels for 0%

commit v1 on v0

--- a/solution.py
+++ b/solution.py
@@ -7,6 +7,11 @@
 KVH = 2
 DH = 128
 TOP = 8
+
+
+def gather_over(x, name, along):
+    sent = jnp.stack([x] * lax.axis_size(name))
+    return jnp.concatenate(lax.all_to_all(sent, name, 0, 0), axis=along)
 
 
 def expert_ffn(slots_in, w_gate, w_up, w_down):
@@ -66,9 +71,7 @@
         jnp.transpose(attended, (2, 0, 1, 3)).reshape(tok_count, HQ * DH).astype(jnp.bfloat16)
     )
     columns = jnp.dot(
-        lax.all_gather(attended, "ctx", axis=0, tiled=True),
-        out_weight,
-        preferred_element_type=jnp.float32,
+        gather_over(attended, "ctx", 0), out_weight, preferred_element_type=jnp.float32
     ).astype(jnp.bfloat16)
     projected = lax.all_to_all(columns, "ctx", split_axis=0, concat_axis=1, tiled=True)
     residual = hidden[0].astype(jnp.float32) + projected.astype(jnp.float32)

time: 839 us -> 809 us (0.964)
  waiting for transfers between devices: 354 us -> 325 us
  between operations: 14.1 us -> 0.68 us
  starting transfers between devices: 15.8 us -> 24.7 us
    all_gather x1 -> x0, waiting for transfers between devices: 119 us -> none  [local(): lax.all_gather(attended, 'ctx', axis=0, tiled=True)]
    all_to_all x0 -> x1, waiting for transfers between devices: none -> 89.5 us  [gather_over(): return jnp.concatenate(lax.all_to_all(sent, name, 0, 0), axis=along)]
where the time goes in v1:
time: 809 us; the launch traced here: 799 us
  waiting for transfers between devices  325 us (40%)
  blocking collectives  252 us (31%)
  local copies, waits for them, and re-layouts  123 us (15%)
  matrix products  49.1 us (6%)
  starting transfers between devices  24.7 us (3%)
  other arithmetic  24.1 us (3%)
    all_to_all x1, waiting for transfers between devices, local(): lax.all_to_all(served, ('dp', 'ctx'), split_axis=0, concat_axis=0, tiled=...  222 us
    all_to_all x1, blocking collectives, local(): lax.all_to_all(outgoing, ('dp', 'ctx'), split_axis=0, concat_axis=0, tile...  197 us
    all_to_all x1, waiting for transfers between devices, gather_over(): return jnp.concatenate(lax.all_to_all(sent, name, 0, 0), axis=along)  89.5 us
    all_gather x1, blocking collectives, local(): value_piece = lax.all_gather(values, 'ctx', axis=1, tiled=True)  29.6 us
    all_gather x1, blocking collectives, local(): key_piece = lax.all_gather(keys, 'ctx', axis=1, tiled=True)  25.4 us
    gather x1, local copies, waits for them, and re-layouts, local(): picked = returned[slot_index].reshape(tok_count, TOP, model_width)  20 us
    scatter x1, local copies, waits for them, and re-layouts, local(): outgoing = jnp.zeros((expert_total * capacity, model_width), jnp.bfloat16...  18.4 us
  transfers between devices with their start and end apart: 3, of which 3 were waited for; matrix products, arithmetic and copies ran while one was open for 1% of the time, Pallas kernels for 0%

profile of v1, /device:TPU:91, one launch (start us, length us, event | category | flops | bytes accessed | tf_op | source)
XLA Modules:
  0.0 799.4 jit_solution(5962564455281677067)
XLA Ops:
  0.0 29.6 %all_gather.7 = bf16[1,1024,256]{2,1,0:T(8,128)(2,1)S(1)} all-gather(bf16[1,128,256]{2,1,0:T(8,128)(2,1)} %param.14), channel_id=1, replica_groups=mesh['dp'=16,'ctx'=8] {'ctx'}, dimensions={1}, use_global_device_ids=true | all-gather | bytes 589824 | tf_op jit(solution)/shard_map/all_gather | solution.py:47
  29.6 0.2 copy.22
  29.9 0.1 iota_compare_fusion.2
  30.0 1.0 copy.19
  30.9 25.4 %all_gather.6 = bf16[1,1024,256]{1,2,0:T(8,128)(2,1)S(1)} all-gather(bf16[1,128,256]{1,2,0:T(8,128)(2,1)S(1)} %copy.19), channel_id=1, replica_groups=mesh['dp'=16,'ctx'=8] {'ctx'}, dimensions={1}, use_global_device_ids=true | all-gather | bytes 589824 | tf_op jit(solution)/shard_map/all_gather | solution.py:46
  56.3 1.5 copy.39
  57.8 2.9 fusion.1
  60.7 4.1 fusion.2
  64.9 4.4 fusion.23
  69.2 0.5 copy.24
  69.8 4.3 stack.2
  74.1 0.0 copy-start.3
  74.1 6.0 all-to-all-start
  80.1 0.0 copy-done.3
  80.1 0.1 copy.28
  80.2 0.1 eq.29
  80.3 0.1 eq.25
  80.4 0.1 copy.27
  80.5 0.1 mul.72
  80.6 0.1 copy.30
  80.7 0.2 fusion.30
  81.0 89.5 %all-to-all-done = bf16[8,128,4096]{2,1,0:T(8,128)(2,1)} async-done(((bf16[8,128,4096]{2,1,0:T(8,128)(2,1)}), bf16[8,128,4096]{2,1,0:T(8,128)(2,1)}, u32[]{:S(2)}, u32[]{:S(2)}) %all-to-all-start) | async-done | bytes 8388640 | tf_op jit(solution)/shard_map/all_to_all | solution.py:14
  170.4 10.0 %convolution_convert_fusion.1 = bf16[1024,512]{1,0:T(8,128)(2,1)} fusion(bf16[1024,4096]{1,0:T(8,128)(2,1)} %bitcast.9, bf16[4096,512]{1,0:T(8,128)(2,1)} %param.15), kind=kOutput, calls=%fused_computation.33 | convolution fusion | flops 4295491584 | bytes 13631488 | tf_op jit(solution)/shard_map/dot_general | solution.py:73
  180.4 0.0 copy-start.1
  180.4 0.0 copy-start.2
  180.4 9.2 %all-to-all-start.1 = ((bf16[8,128,512]{2,1,0:T(8,128)(2,1)}), bf16[8,128,512]{2,1,0:T(8,128)(2,1)S(1)}, u32[]{:S(2)}, u32[]{:S(2)}) async-start(bf16[8,128,512]{2,1,0:T(8,128)(2,1)} %bitcast.93), calls=%async_computation.1 | async-start | bytes 2097152 | tf_op jit(solution)/shard_map/all_to_all | solution.py:76
  189.7 0.1 copy.31
  189.8 0.4 fusion.29
  190.2 13.5 %all-to-all-done.1 = bf16[8,128,512]{2,1,0:T(8,128)(2,1)S(1)} async-done(((bf16[8,128,512]{2,1,0:T(8,128)(2,1)}), bf16[8,128,512]{2,1,0:T(8,128)(2,1)S(1)}, u32[]{:S(2)}, u32[]{:S(2)}) %all-to-all-start.1) | async-done | bytes 1048608 | tf_op jit(solution)/shard_map/all_to_all | solution.py:76
  203.7 1.6 convert_bitcast_fusion
  205.3 0.2 copy.38
  205.6 0.0 copy-done.1
  205.6 0.4 multiply_reduce_fusion
  206.0 0.0 copy-done.2
  206.0 0.4 multiply_convert_fusion
  206.4 7.7 gather_fusion
  214.2 18.4 %scatter_custom_fusion = bf16[1152,4096]{1,0:T(8,128)(2,1)} fusion(s32[1024]{0:T(1024)S(1)} %bitcast.97, bf16[1024,4096]{1,0:T(8,128)(2,1)} %gather_fusion, bf16[]{:T(256)} %constant.43.clone.1), kind=kCustom, calls=%fused_computation.18 | custom fusion | bytes 9437696 | tf_op jit(solution)/shard_map/scatter | solution.py:97
  232.5 15.1 %reshape.170 = bf16[128,9,4096]{2,1,0:T(8,128)(2,1)} reshape(bf16[1152,4096]{1,0:T(8,128)(2,1)} %scatter_custom_fusion) | data formatting | bytes 18874368 | tf_op jit(solution)/shard_map/reshape | solution.py:99
  247.7 197.3 %all_to_all.28 = bf16[128,9,4096]{2,1,0:T(8,128)(2,1)} all-to-all(bf16[128,9,4096]{2,1,0:T(8,128)(2,1)} %reshape.170), channel_id=1, replica_groups=mesh['dp'=16,'ctx'=8] {'dp','ctx'}, dimensions={0} | all-to-all | bytes 18874368 | tf_op jit(solution)/shard_map/all_to_all | solution.py:101
  445.0 15.8 %reshape.171 = bf16[1152,4096]{1,0:T(8,128)(2,1)} reshape(bf16[128,9,4096]{2,1,0:T(8,128)(2,1)} %all_to_all.28) | data formatting | bytes 18874368 | tf_op jit(solution)/shard_map/reshape | solution.py:18
  460.8 0.0 copy-start
  460.8 0.0 slice-start
  460.8 12.0 %fusion.10 = f32[1152,768]{1,0:T(8,128)S(1)} fusion(bf16[1152,4096]{1,0:T(8,128)(2,1)} %reshape.171, bf16[1,4096,768]{2,1,0:T(8,128)(2,1)} %param.19), kind=kOutput, calls=%fused_computation.16 | convolution fusion | flops 7247757312 | bytes 19267584 | tf_op jit(solution)/shard_map/dot_general | solution.py:19
  472.8 0.0 copy-done
  472.8 0.0 slice-start.1
  472.8 10.3 %fusion.17 = bf16[1152,768]{1,0:T(8,128)(2,1)S(1)} fusion(bf16[1152,4096]{1,0:T(8,128)(2,1)S(1)} %copy-done, bf16[1,4096,768]{2,1,0:T(8,128)(2,1)} %param.20, f32[1152,768]{1,0:T(8,128)S(1)} %fusion.10), kind=kOutput, calls=%fused_computation.21 | convolution fusion | flops 7253065728 | bytes 21037056 | tf_op jit(solution)/shard_map/dot_general | solution.py:20
  483.1 0.0 slice-done
  483.1 0.0 slice-done.1
  483.1 9.6 %convolution_convert_fusion = bf16[1152,4096]{1,0:T(8,128)(2,1)} fusion(bf16[1152,768]{1,0:T(8,128)(2,1)S(1)} %fusion.17, bf16[1,768,4096]{2,1,0:T(8,128)(2,1)S(1)} %bitcast.102), kind=kOutput, calls=%fused_computation.7 | convolution fusion | flops 7252475904 | bytes 17498112 | tf_op jit(solution)/shard_map/dot_general | solution.py:22
  492.7 15.1 %reshape.172 = bf16[128,9,4096]{2,1,0:T(8,128)(2,1)} reshape(bf16[1152,4096]{1,0:T(8,128)(2,1)} %convolution_convert_fusion) | data formatting | bytes 18874368 | tf_op jit(solution)/shard_map/reshape | solution.py:23
  507.8 0.0 copy-start.4
  507.8 9.5 %all-to-all-start.3 = ((bf16[128,9,4096]{2,1,0:T(8,128)(2,1)}), bf16[128,9,4096]{2,1,0:T(8,128)(2,1)}, u32[]{:S(2)}, u32[]{:S(2)}) async-start(bf16[128,9,4096]{2,1,0:T(8,128)(2,1)} %reshape.172), calls=%async_computation.3 | async-start | bytes 33554432 | tf_op jit(solution)/shard_map/all_to_all | solution.py:106
  517.4 0.0 copy-done.4
  517.4 0.1 copy.26
  517.5 4.2 copy.25
  521.7 2.7 reshape.174
  524.4 222.0 %all-to-all-done.3 = bf16[128,9,4096]{2,1,0:T(8,128)(2,1)} async-done(((bf16[128,9,4096]{2,1,0:T(8,128)(2,1)}), bf16[128,9,4096]{2,1,0:T(8,128)(2,1)}, u32[]{:S(2)}, u32[]{:S(2)}) %all-to-all-start.3) | async-done | bytes 9437216 | tf_op jit(solution)/shard_map/all_to_all | solution.py:106
  746.5 15.8 %reshape.173 = bf16[1152,4096]{1,0:T(8,128)(2,1)} reshape(bf16[128,9,4096]{2,1,0:T(8,128)(2,1)} %all-to-all-done.3) | data formatting | bytes 18874368 | tf_op jit(solution)/shard_map/reshape | solution.py:107
  762.3 20.0 %gather_fusion.1 = bf16[1024,4096]{1,0:T(8,128)(2,1)} fusion(bf16[1152,4096]{1,0:T(8,128)(2,1)} %reshape.173, s32[1024]{0:T(1024)S(1)} %broadcast_clamp_fusion), kind=kCustom, calls=%fused_computation.1 | custom fusion | bytes 16781312 | tf_op jit(solution)/shard_map/gather | solution.py:108
  782.3 13.2 %fusion = f32[128,4096]{1,0:T(8,128)} fusion(bf16[1024,4096]{1,0:T(8,128)(2,1)} %gather_fusion.1, f32[128,8]{1,0:T(8,128)S(1)} %copy.26), kind=kLoop, calls=%fused_computation.4 | loop fusion | flops 12058624 | bytes 10489856 | tf_op jit(solution)/shard_map/reduce_sum | solution.py:109
  795.5 3.5 fusion.21
  (15 shorter events, 0.1 us)
Async XLA Ops:
  74.1 6.0 copy-start.3
  74.1 96.3 %all-to-all-start = ((bf16[8,128,4096]{2,1,0:T(8,128)(2,1)}), bf16[8,128,4096]{2,1,0:T(8,128)(2,1)}, u32[]{:S(2)}, u32[]{:S(2)}) async-start(bf16[8,128,4096]{2,1,0:T(8,128)(2,1)} %stack.2), calls=%async_computation | async-start | bytes 16777216 | tf_op jit(solution)/shard_map/all_to_all | solution.py:14
  180.4 25.1 %copy-start.1 = (bf16[1,128,4096]{2,1,0:T(8,128)(2,1)S(1)}, bf16[1,128,4096]{2,1,0:T(8,128)(2,1)}, u32[]{:S(2)}) copy-start(bf16[1,128,4096]{2,1,0:T(8,128)(2,1)} %param.11) | copy-start | bytes 3145732
  180.4 25.6 %copy-start.2 = (f32[4096]{0:T(1024)S(1)}, f32[4096]{0:T(1024)}, u32[]{:S(2)}) copy-start(f32[4096]{0:T(1024)} %param.16) | copy-start | bytes 49156
  180.4 23.3 %all-to-all-start.1 = ((bf16[8,128,512]{2,1,0:T(8,128)(2,1)}), bf16[8,128,512]{2,1,0:T(8,128)(2,1)S(1)}, u32[]{:S(2)}, u32[]{:S(2)}) async-start(bf16[8,128,512]{2,1,0:T(8,128)(2,1)} %bitcast.93), calls=%async_computation.1 | async-start | bytes 2097152 | tf_op jit(solution)/shard_map/all_to_all | solution.py:76
  460.8 12.0 %copy-start = (bf16[1152,4096]{1,0:T(8,128)(2,1)S(1)}, bf16[1152,4096]{1,0:T(8,128)(2,1)}, u32[]{:S(2)}) copy-start(bf16[1152,4096]{1,0:T(8,128)(2,1)} %reshape.171) | copy-start | bytes 28311556
  460.8 22.3 %slice-start = ((s8[6291456]{0:T(1024)(128)(4,1)}), s8[4194304]{0:T(1024)(128)(4,1)S(1)}, s32[]{:S(2)}) async-start(s8[6291456]{0:T(1024)(128)(4,1)} %bitcast.101), calls=%async_computation.4 | async-start | bytes 8388608
  472.8 10.3 %slice-start.1 = ((s8[6291456]{0:T(1024)(128)(4,1)}), s8[2097152]{0:T(1024)(128)(4,1)S(1)}, s32[]{:S(2)}) async-start(s8[6291456]{0:T(1024)(128)(4,1)} %bitcast.101), calls=%async_computation.5 | async-start | bytes 4194304
  507.8 9.6 %copy-start.4 = (f32[1,128,8]{1,2,0:T(8,128)S(1)}, f32[1,128,8]{1,2,0:T(8,128)}, u32[]{:S(2)}) copy-start(f32[1,128,8]{1,2,0:T(8,128)} %param.18) | copy-start | bytes 12292
  507.8 238.7 %all-to-all-start.3 = ((bf16[128,9,4096]{2,1,0:T(8,128)(2,1)}), bf16[128,9,4096]{2,1,0:T(8,128)(2,1)}, u32[]{:S(2)}, u32[]{:S(2)}) async-start(bf16[128,9,4096]{2,1,0:T(8,128)(2,1)} %reshape.172), calls=%async_computation.3 | async-start | bytes 33554432 | tf_op jit(solution)/shard_map/all_to_all | solution.py:106
